TPU v7x, 512 devices: a whole 4x4x16 slice. The times are simulated.
512 devices in a mesh: chan: 64 (over y, x, z_hi, core), freq: 8 (over z_lo).
Axes of the slice: x: 4, y: 4, z: 16 (z_hi: 2, z_lo: 8; z = z_hi * 8 + z_lo), core: 2. Of those that a mesh axis runs over, the one named last changes fastest.
Arguments:
- spectra: bfloat16 [256, 2, 16, 8192], P('freq', None, None, 'chan'), may hold values from -20 to 20
- model: bfloat16 [256, 2, 8, 8192], P('freq', None, None, 'chan'), may hold values from -6 to 6
- channel_ok: int32 [8192], replicated, may hold values 0 or 1
- limits: int32 [64], replicated, may hold values from 128 to 1024, as said below
Outputs:
- adjoint: float32 [256, 2, 16, 8192], P('freq', None, None, 'chan')
- misfit: float32 [], replicated
Inputs may be any that keep to these rules, and one draw needn't show every extreme that they name: `limits`: one block has the limit 128 and another the limit 1024.
All inputs are finite; a program needn't handle non-finite values.
Results may differ from a plain program's by a relative error of at most 0.00053.
Values may be sent and summed in bfloat16 or wider, within the bound.
A program may use at most 64 MiB of HBM per device.

v0:
```python
import jax
import jax.numpy as jnp
from jax import lax
from jax.sharding import PartitionSpec as P

F = 256
W = 16
BAND = 1024


def shifted(x, axis, by):
    peers = lax.axis_size(axis)
    return lax.ppermute(x, axis, [(i, (i + by) % peers) for i in range(peers)])


def pair_terms(first_block, second_block, ok_first, ok_second, limit_first, shift_blocks):
    bin_count = first_block.shape[0]
    row_count = first_block.shape[2]
    block_width = first_block.shape[3]
    row_scale = jnp.concatenate(
        [jnp.full((W,), 1.0 / W, jnp.float32), jnp.full((row_count - W,), -1.0, jnp.float32)]
    ).astype(jnp.bfloat16)
    scaled = first_block * row_scale[None, None, :, None]
    stacked_left = jnp.stack(
        [
            scaled.reshape(bin_count, 2 * row_count, block_width),
            jnp.concatenate([scaled[:, 1], -scaled[:, 0]], axis=1),
        ],
        axis=0,
    )
    right_rows = second_block.reshape(bin_count, 2 * row_count, block_width)
    cross_spec = jnp.einsum(
        "xfrc,frd->xfcd", stacked_left, right_rows, preferred_element_type=jnp.float32
    )
    row_index = lax.broadcasted_iota(jnp.int32, (block_width, block_width), 0)
    col_index = lax.broadcasted_iota(jnp.int32, (block_width, block_width), 1)
    offset = shift_blocks * block_width + col_index - row_index
    inside = ((offset >= 1) & (offset <= limit_first)).astype(jnp.float32)
    live_mask = ok_first[:, None] * ok_second[None, :] * inside
    residual = cross_spec * live_mask[None, None]
    piece_loss = 0.5 * jnp.sum(residual * residual)
    rounded = residual.astype(jnp.bfloat16)
    far_spec = second_block[:, :, :W].reshape(bin_count, 2 * W, block_width)
    near_spec = first_block[:, :, :W].reshape(bin_count, 2 * W, block_width)
    toward = jnp.einsum("xfcd,fvd->xfvc", rounded, far_spec, preferred_element_type=jnp.float32)
    first_real = toward[0, :, :W] - toward[1, :, W:]
    first_imag = toward[0, :, W:] + toward[1, :, :W]
    backward = jnp.einsum("xfcd,fvc->xfvd", rounded, near_spec, preferred_element_type=jnp.float32)
    second_real = backward[0, :, :W] + backward[1, :, W:]
    second_imag = backward[0, :, W:] - backward[1, :, :W]
    return (
        piece_loss,
        jnp.stack([first_real, first_imag], axis=1),
        jnp.stack([second_real, second_imag], axis=1),
    )


def shards(spectra, model, channel_ok, limits):
    payload = jnp.concatenate([spectra, model], axis=2)
    block_width = spectra.shape[3]
    band_blocks = BAND // block_width
    block_total = lax.axis_size("chan")
    block_index = lax.axis_index("chan")
    ok_all = channel_ok.astype(jnp.float32)

    def flags_of(move):
        start = (block_index + move) % block_total * block_width
        return lax.dynamic_slice_in_dim(ok_all, start, block_width)

    ok_own = flags_of(0)
    limit_own = lax.dynamic_index_in_dim(limits, block_index % block_total, keepdims=False)
    misfit_sum, near_terms, far_terms = pair_terms(payload, payload, ok_own, ok_own, limit_own, 0)
    adjoint_acc = near_terms + far_terms
    for s in range(1, band_blocks + 1):
        ahead_block = shifted(payload, "chan", -s)
        piece_loss, near_terms, far_terms = pair_terms(
            payload, ahead_block, ok_own, flags_of(s), limit_own, s
        )
        misfit_sum = misfit_sum + piece_loss
        adjoint_acc = adjoint_acc + near_terms
        adjoint_acc = adjoint_acc + shifted(far_terms, "chan", s)
    misfit_total = lax.psum(misfit_sum, ("chan", "freq"))
    misfit = misfit_total / float(F * block_width * block_total * BAND)
    return (adjoint_acc * (1.0 / W), misfit)


def solution(mesh):
    return jax.shard_map(
        shards,
        mesh=mesh,
        in_specs=(P("freq", None, None, "chan"), P("freq", None, None, "chan"), P(), P()),
        out_specs=(P("freq", None, None, "chan"), P()),
        check_vma=False,
    )
```

profile of v0, /device:TPU:104, one launch (start us, length us, event | category | flops | bytes accessed | tf_op | source)
XLA Modules:
  0.0 482.6 jit_solution(15571919331790536662)
XLA Ops:
  0.7 1.0 constant_dynamic-update-slice_fusion.1
  1.6 0.9 constant_dynamic-update-slice_fusion
  2.6 1.5 broadcast_multiply_fusion
  4.0 4.8 collective-permute-start.14
  8.8 1.9 collective-permute-start.12
  10.8 17.6 %collective-permute-start.10 = (bf16[32,2,24,128]{3,2,0,1:T(8,128)(2,1)}, bf16[32,2,24,128]{3,2,0,1:T(8,128)(2,1)S(1)}, u32[]{:S(2)}, u32[]{:S(2)}) collective-permute-start(bf16[32,2,24,128]{3,2,0,1:T(8,128)(2,1)} %get-tuple-element.61), channel_id=1, source_target_pairs={{0,464},{8,472},{16,480},{24,488},{32,496},{40,504},{48,0},{56,8},... | collective-permute-start | bytes 1179656 | tf_op jit(solution)/shard_map/ppermute | solution.py:13
  28.4 12.3 %collective-permute-start.8 = (bf16[32,2,24,128]{3,2,0,1:T(8,128)(2,1)}, bf16[32,2,24,128]{3,2,0,1:T(8,128)(2,1)S(1)}, u32[]{:S(2)}, u32[]{:S(2)}) collective-permute-start(bf16[32,2,24,128]{3,2,0,1:T(8,128)(2,1)} %get-tuple-element.61), channel_id=1, source_target_pairs={{0,472},{8,480},{16,488},{24,496},{32,504},{40,0},{48,8},{56,16},{... | collective-permute-start | bytes 1179656 | tf_op jit(solution)/shard_map/ppermute | solution.py:13
  40.7 3.0 collective-permute-start.6
  45.0 1.0 multiply_select_fusion.8
  46.0 1.9 multiply_reduce_fusion.8
  47.9 0.8 fusion.91
  49.2 0.8 fusion.144
  50.0 1.9 collective-permute-start.4
  51.9 1.9 multiply_reduce_fusion
  53.8 0.8 fusion.88
  55.2 0.8 fusion.114
  56.0 1.9 collective-permute-start.2
  57.9 2.0 multiply_reduce_fusion.1
  59.9 0.8 fusion.82
  61.2 0.9 fusion.118
  62.1 56.0 %collective-permute-start = (bf16[32,2,24,128]{3,2,0,1:T(8,128)(2,1)}, bf16[32,2,24,128]{3,2,0,1:T(8,128)(2,1)S(1)}, u32[]{:S(2)}, u32[]{:S(2)}) collective-permute-start(bf16[32,2,24,128]{3,2,0,1:T(8,128)(2,1)} %get-tuple-element.61), channel_id=1, source_target_pairs={{0,504},{8,0},{16,8},{24,16},{32,24},{40,32},{48,40},{56,48},{64,5... | collective-permute-start | bytes 1179656 | tf_op jit(solution)/shard_map/ppermute | solution.py:13
  118.2 2.0 multiply_reduce_fusion.2
  120.1 0.8 fusion.76
  121.5 0.8 pad_maximum_fusion.8
  122.3 0.9 fusion.122
  123.2 12.3 %collective-permute-start.15 = (f32[32,2,16,128]{3,2,0,1:T(8,128)}, f32[32,2,16,128]{3,2,0,1:T(8,128)}, u32[]{:S(2)}, u32[]{:S(2)}) collective-permute-start(f32[32,2,16,128]{3,2,0,1:T(8,128)} %pad_maximum_fusion.8), channel_id=1, source_target_pairs={{0,64},{8,72},{16,80},{24,88},{32,96},{40,104},{48,112},{56,120},{... | collective-permute-start | bytes 1572872 | tf_op jit(solution)/shard_map/ppermute | solution.py:13
  135.6 2.0 multiply_reduce_fusion.3
  137.6 0.8 fusion.70
  138.9 0.9 pad_maximum_fusion.7
  139.8 0.9 fusion.126
  140.7 1.9 collective-permute-start.13
  142.6 2.0 multiply_reduce_fusion.4
  144.6 0.8 fusion.64
  145.9 0.8 pad_maximum_fusion.6
  146.8 0.9 fusion.130
  147.7 1.9 collective-permute-start.11
  149.6 1.9 multiply_reduce_fusion.5
  151.6 0.8 fusion.58
  152.4 0.9 fusion.132
  153.3 0.9 pad_maximum_fusion.5
  154.6 6.8 %collective-permute-start.9 = (f32[32,2,16,128]{3,2,0,1:T(8,128)}, f32[32,2,16,128]{3,2,0,1:T(8,128)}, u32[]{:S(2)}, u32[]{:S(2)}) collective-permute-start(f32[32,2,16,128]{3,2,0,1:T(8,128)} %pad_maximum_fusion.5), channel_id=1, source_target_pairs={{0,40},{8,48},{16,56},{24,64},{32,72},{40,80},{48,88},{56,96},{64,... | collective-permute-start | bytes 1572872 | tf_op jit(solution)/shard_map/ppermute | solution.py:13
  161.5 1.9 multiply_reduce_fusion.6
  163.4 0.8 fusion.52
  164.2 0.9 fusion.134
  165.1 0.7 copy.62
  165.8 0.8 pad_maximum_fusion.4
  166.6 0.9 fusion.136
  167.5 19.7 %collective-permute-start.7 = (f32[32,2,16,128]{3,2,0,1:T(8,128)}, f32[32,2,16,128]{3,2,0,1:T(8,128)}, u32[]{:S(2)}, u32[]{:S(2)}) collective-permute-start(f32[32,2,16,128]{3,2,0,1:T(8,128)} %pad_maximum_fusion.4), channel_id=1, source_target_pairs={{0,32},{8,40},{16,48},{24,56},{32,64},{40,72},{48,80},{56,88},{64,... | collective-permute-start | bytes 1572872 | tf_op jit(solution)/shard_map/ppermute | solution.py:13
  187.3 2.0 multiply_reduce_fusion.7
  189.2 0.8 fusion.46
  190.0 0.9 fusion.140
  197.4 166.3 %psum.7 = f32[]{:T(128)} all-reduce(f32[]{:T(128)S(6)} %add.578), channel_id=1, replica_groups=mesh['chan'=64,'freq'=8] {'chan','freq'}, use_global_device_ids=true, to_apply=%region_9.10 | all-reduce | flops 1 | bytes 8 | tf_op jit(solution)/shard_map/psum | solution.py:82
  363.7 1.9 pad_maximum_fusion.3
  365.6 1.9 pad_maximum_fusion.2
  367.5 0.9 pad_maximum_fusion.1
  369.1 1.5 fusion.49
  370.7 8.0 %collective-permute-start.5 = (f32[32,2,16,128]{3,2,0,1:T(8,128)S(1)}, f32[32,2,16,128]{3,2,0,1:T(8,128)S(1)}, u32[]{:S(2)}, u32[]{:S(2)}) collective-permute-start(f32[32,2,16,128]{3,2,0,1:T(8,128)S(1)} %copy-done.18), channel_id=1, source_target_pairs={{0,24},{8,32},{16,40},{24,48},{32,56},{40,64},{48,72},{56,80},{64,... | collective-permute-start | bytes 1572872 | tf_op jit(solution)/shard_map/ppermute | solution.py:13
  378.7 4.5 collective-permute-start.3
  383.2 1.9 collective-permute-start.1
  385.8 37.9 %collective-permute-done.5 = f32[32,2,16,128]{3,2,0,1:T(8,128)S(1)} collective-permute-done((f32[32,2,16,128]{3,2,0,1:T(8,128)S(1)}, f32[32,2,16,128]{3,2,0,1:T(8,128)S(1)}, u32[]{:S(2)}, u32[]{:S(2)}) %collective-permute-start.5) | collective-permute-done | bytes 524320 | tf_op jit(solution)/shard_map/ppermute | solution.py:13
  423.7 48.4 %collective-permute-done.3 = f32[32,2,16,128]{3,2,0,1:T(8,128)S(1)} collective-permute-done((f32[32,2,16,128]{3,2,0,1:T(8,128)S(1)}, f32[32,2,16,128]{3,2,0,1:T(8,128)S(1)}, u32[]{:S(2)}, u32[]{:S(2)}) %collective-permute-start.3) | collective-permute-done | bytes 524320 | tf_op jit(solution)/shard_map/ppermute | solution.py:13
  472.2 6.0 %collective-permute-done.1 = f32[32,2,16,128]{3,2,0,1:T(8,128)S(1)} collective-permute-done((f32[32,2,16,128]{3,2,0,1:T(8,128)S(1)}, f32[32,2,16,128]{3,2,0,1:T(8,128)S(1)}, u32[]{:S(2)}, u32[]{:S(2)}) %collective-permute-start.1) | collective-permute-done | bytes 524320 | tf_op jit(solution)/shard_map/ppermute | solution.py:13
  478.3 2.3 fusion.110
  480.6 0.9 copy.104
  (113 shorter events, 6.4 us)
Async XLA Ops:
  0.6 43.4 %copy-start.22 = (bf16[24]{0:T(256)(128)(2,1)S(1)}, bf16[24]{0:T(256)(128)(2,1)}, u32[]{:S(2)}) copy-start(bf16[24]{0:T(256)(128)(2,1)} %constant.88.clone.1) | copy-start | bytes 148
  0.6 43.3 %copy-start.21 = (s32[8192]{0:T(1024)S(1)}, s32[8192]{0:T(1024)}, u32[]{:S(2)}) copy-start(s32[8192]{0:T(1024)} %param.6) | copy-start | bytes 98308
  0.7 43.5 %copy-start.23 = (s32[64]{0:T(128)S(1)}, s32[64]{0:T(128)}, u32[]{:S(2)}) copy-start(s32[64]{0:T(128)} %param.7) | copy-start | bytes 772
  4.0 45.9 %collective-permute-start.14 = (bf16[32,2,24,128]{3,2,0,1:T(8,128)(2,1)}, bf16[32,2,24,128]{3,2,0,1:T(8,128)(2,1)S(1)}, u32[]{:S(2)}, u32[]{:S(2)}) collective-permute-start(bf16[32,2,24,128]{3,2,0,1:T(8,128)(2,1)} %get-tuple-element.61), channel_id=1, source_target_pairs={{0,448},{8,456},{16,464},{24,472},{32,480},{40,488},{48,496},{56,5... | collective-permute-start | bytes 1179656 | tf_op jit(solution)/shard_map/ppermute | solution.py:13
  8.8 47.1 %collective-permute-start.12 = (bf16[32,2,24,128]{3,2,0,1:T(8,128)(2,1)}, bf16[32,2,24,128]{3,2,0,1:T(8,128)(2,1)S(1)}, u32[]{:S(2)}, u32[]{:S(2)}) collective-permute-start(bf16[32,2,24,128]{3,2,0,1:T(8,128)(2,1)} %get-tuple-element.61), channel_id=1, source_target_pairs={{0,456},{8,464},{16,472},{24,480},{32,488},{40,496},{48,504},{56,0... | collective-permute-start | bytes 1179656 | tf_op jit(solution)/shard_map/ppermute | solution.py:13
  10.8 51.3 %collective-permute-start.10 = (bf16[32,2,24,128]{3,2,0,1:T(8,128)(2,1)}, bf16[32,2,24,128]{3,2,0,1:T(8,128)(2,1)S(1)}, u32[]{:S(2)}, u32[]{:S(2)}) collective-permute-start(bf16[32,2,24,128]{3,2,0,1:T(8,128)(2,1)} %get-tuple-element.61), channel_id=1, source_target_pairs={{0,464},{8,472},{16,480},{24,488},{32,496},{40,504},{48,0},{56,8},... | collective-permute-start | bytes 1179656 | tf_op jit(solution)/shard_map/ppermute | solution.py:13
  28.4 94.8 %collective-permute-start.8 = (bf16[32,2,24,128]{3,2,0,1:T(8,128)(2,1)}, bf16[32,2,24,128]{3,2,0,1:T(8,128)(2,1)S(1)}, u32[]{:S(2)}, u32[]{:S(2)}) collective-permute-start(bf16[32,2,24,128]{3,2,0,1:T(8,128)(2,1)} %get-tuple-element.61), channel_id=1, source_target_pairs={{0,472},{8,480},{16,488},{24,496},{32,504},{40,0},{48,8},{56,16},{... | collective-permute-start | bytes 1179656 | tf_op jit(solution)/shard_map/ppermute | solution.py:13
  40.7 100.0 %collective-permute-start.6 = (bf16[32,2,24,128]{3,2,0,1:T(8,128)(2,1)}, bf16[32,2,24,128]{3,2,0,1:T(8,128)(2,1)S(1)}, u32[]{:S(2)}, u32[]{:S(2)}) collective-permute-start(bf16[32,2,24,128]{3,2,0,1:T(8,128)(2,1)} %get-tuple-element.61), channel_id=1, source_target_pairs={{0,480},{8,488},{16,496},{24,504},{32,0},{40,8},{48,16},{56,24},{6... | collective-permute-start | bytes 1179656 | tf_op jit(solution)/shard_map/ppermute | solution.py:13
  46.0 1.9 copy-start
  50.0 97.7 %collective-permute-start.4 = (bf16[32,2,24,128]{3,2,0,1:T(8,128)(2,1)}, bf16[32,2,24,128]{3,2,0,1:T(8,128)(2,1)S(1)}, u32[]{:S(2)}, u32[]{:S(2)}) collective-permute-start(bf16[32,2,24,128]{3,2,0,1:T(8,128)(2,1)} %get-tuple-element.61), channel_id=1, source_target_pairs={{0,488},{8,496},{16,504},{24,0},{32,8},{40,16},{48,24},{56,32},{64... | collective-permute-start | bytes 1179656 | tf_op jit(solution)/shard_map/ppermute | solution.py:13
  56.0 98.6 %collective-permute-start.2 = (bf16[32,2,24,128]{3,2,0,1:T(8,128)(2,1)}, bf16[32,2,24,128]{3,2,0,1:T(8,128)(2,1)S(1)}, u32[]{:S(2)}, u32[]{:S(2)}) collective-permute-start(bf16[32,2,24,128]{3,2,0,1:T(8,128)(2,1)} %get-tuple-element.61), channel_id=1, source_target_pairs={{0,496},{8,504},{16,0},{24,8},{32,16},{40,24},{48,32},{56,40},{64,... | collective-permute-start | bytes 1179656 | tf_op jit(solution)/shard_map/ppermute | solution.py:13
  62.1 105.4 %collective-permute-start = (bf16[32,2,24,128]{3,2,0,1:T(8,128)(2,1)}, bf16[32,2,24,128]{3,2,0,1:T(8,128)(2,1)S(1)}, u32[]{:S(2)}, u32[]{:S(2)}) collective-permute-start(bf16[32,2,24,128]{3,2,0,1:T(8,128)(2,1)} %get-tuple-element.61), channel_id=1, source_target_pairs={{0,504},{8,0},{16,8},{24,16},{32,24},{40,32},{48,40},{56,48},{64,5... | collective-permute-start | bytes 1179656 | tf_op jit(solution)/shard_map/ppermute | solution.py:13
  123.2 247.5 %collective-permute-start.15 = (f32[32,2,16,128]{3,2,0,1:T(8,128)}, f32[32,2,16,128]{3,2,0,1:T(8,128)}, u32[]{:S(2)}, u32[]{:S(2)}) collective-permute-start(f32[32,2,16,128]{3,2,0,1:T(8,128)} %pad_maximum_fusion.8), channel_id=1, source_target_pairs={{0,64},{8,72},{16,80},{24,88},{32,96},{40,104},{48,112},{56,120},{... | collective-permute-start | bytes 1572872 | tf_op jit(solution)/shard_map/ppermute | solution.py:13
  140.7 238.0 %collective-permute-start.13 = (f32[32,2,16,128]{3,2,0,1:T(8,128)}, f32[32,2,16,128]{3,2,0,1:T(8,128)}, u32[]{:S(2)}, u32[]{:S(2)}) collective-permute-start(f32[32,2,16,128]{3,2,0,1:T(8,128)} %pad_maximum_fusion.7), channel_id=1, source_target_pairs={{0,56},{8,64},{16,72},{24,80},{32,88},{40,96},{48,104},{56,112},{6... | collective-permute-start | bytes 1572872 | tf_op jit(solution)/shard_map/ppermute | solution.py:13
  147.7 235.5 %collective-permute-start.11 = (f32[32,2,16,128]{3,2,0,1:T(8,128)}, f32[32,2,16,128]{3,2,0,1:T(8,128)}, u32[]{:S(2)}, u32[]{:S(2)}) collective-permute-start(f32[32,2,16,128]{3,2,0,1:T(8,128)} %pad_maximum_fusion.6), channel_id=1, source_target_pairs={{0,48},{8,56},{16,64},{24,72},{32,80},{40,88},{48,96},{56,104},{64... | collective-permute-start | bytes 1572872 | tf_op jit(solution)/shard_map/ppermute | solution.py:13
  154.6 231.2 %collective-permute-start.9 = (f32[32,2,16,128]{3,2,0,1:T(8,128)}, f32[32,2,16,128]{3,2,0,1:T(8,128)}, u32[]{:S(2)}, u32[]{:S(2)}) collective-permute-start(f32[32,2,16,128]{3,2,0,1:T(8,128)} %pad_maximum_fusion.5), channel_id=1, source_target_pairs={{0,40},{8,48},{16,56},{24,64},{32,72},{40,80},{48,88},{56,96},{64,... | collective-permute-start | bytes 1572872 | tf_op jit(solution)/shard_map/ppermute | solution.py:13
  167.5 218.3 %collective-permute-start.7 = (f32[32,2,16,128]{3,2,0,1:T(8,128)}, f32[32,2,16,128]{3,2,0,1:T(8,128)}, u32[]{:S(2)}, u32[]{:S(2)}) collective-permute-start(f32[32,2,16,128]{3,2,0,1:T(8,128)} %pad_maximum_fusion.4), channel_id=1, source_target_pairs={{0,32},{8,40},{16,48},{24,56},{32,64},{40,72},{48,80},{56,88},{64,... | collective-permute-start | bytes 1572872 | tf_op jit(solution)/shard_map/ppermute | solution.py:13
  189.2 1.7 copy-start.1
  196.7 170.8 %copy-start.15 = (f32[32,1,16,128]{3,2,0,1:T(8,128)S(1)}, f32[32,1,16,128]{3,2,0,1:T(8,128)}, u32[]{:S(2)}) copy-start(f32[32,1,16,128]{3,2,0,1:T(8,128)} %get-tuple-element.28) | copy-start | bytes 786436
  363.7 3.8 copy-start.16
  369.0 1.6 copy-start.18
  369.0 9.7 %copy-start.19 = (f32[32,2,16,128]{3,2,0,1:T(8,128)S(1)}, f32[32,2,16,128]{3,2,0,1:T(8,128)}, u32[]{:S(2)}) copy-start(f32[32,2,16,128]{3,2,0,1:T(8,128)} %pad_maximum_fusion.2) | copy-start | bytes 1572868
  369.0 14.2 %copy-start.20 = (f32[32,2,16,128]{3,2,0,1:T(8,128)S(1)}, f32[32,2,16,128]{3,2,0,1:T(8,128)}, u32[]{:S(2)}) copy-start(f32[32,2,16,128]{3,2,0,1:T(8,128)} %pad_maximum_fusion.1) | copy-start | bytes 1572868
  369.1 16.1 %copy-start.2 = (bf16[2,32,128,128]{2,3,0,1:T(8,128)(2,1)S(1)}, bf16[2,32,128,128]{2,3,0,1:T(8,128)(2,1)}, u32[]{:S(2)}) copy-start(bf16[2,32,128,128]{2,3,0,1:T(8,128)(2,1)} %copy-done.1) | copy-start | bytes 6291460
  369.1 16.1 %copy-start.17 = (bf16[32,2,16,128]{3,2,1,0:T(8,128)(2,1)S(1)}, bf16[32,2,16,128]{3,2,1,0:T(8,128)(2,1)}, u32[]{:S(2)}) copy-start(bf16[32,2,16,128]{3,2,1,0:T(8,128)(2,1)} %copy.56) | copy-start | bytes 786436
  370.7 53.0 %collective-permute-start.5 = (f32[32,2,16,128]{3,2,0,1:T(8,128)S(1)}, f32[32,2,16,128]{3,2,0,1:T(8,128)S(1)}, u32[]{:S(2)}, u32[]{:S(2)}) collective-permute-start(f32[32,2,16,128]{3,2,0,1:T(8,128)S(1)} %copy-done.18), channel_id=1, source_target_pairs={{0,24},{8,32},{16,40},{24,48},{32,56},{40,64},{48,72},{56,80},{64,... | collective-permute-start | bytes 1572872 | tf_op jit(solution)/shard_map/ppermute | solution.py:13
  378.7 93.5 %collective-permute-start.3 = (f32[32,2,16,128]{3,2,0,1:T(8,128)S(1)}, f32[32,2,16,128]{3,2,0,1:T(8,128)S(1)}, u32[]{:S(2)}, u32[]{:S(2)}) collective-permute-start(f32[32,2,16,128]{3,2,0,1:T(8,128)S(1)} %copy-done.19), channel_id=1, source_target_pairs={{0,16},{8,24},{16,32},{24,40},{32,48},{40,56},{48,64},{56,72},{64,... | collective-permute-start | bytes 1572872 | tf_op jit(solution)/shard_map/ppermute | solution.py:13
  383.2 95.0 %collective-permute-start.1 = (f32[32,2,16,128]{3,2,0,1:T(8,128)S(1)}, f32[32,2,16,128]{3,2,0,1:T(8,128)S(1)}, u32[]{:S(2)}, u32[]{:S(2)}) collective-permute-start(f32[32,2,16,128]{3,2,0,1:T(8,128)S(1)} %copy-done.20), channel_id=1, source_target_pairs={{0,8},{8,16},{16,24},{24,32},{32,40},{40,48},{48,56},{56,64},{64,7... | collective-permute-start | bytes 1572872 | tf_op jit(solution)/shard_map/ppermute | solution.py:13
  385.2 93.0 %copy-start.3 = (f32[32,1,16,128]{3,2,0,1:T(8,128)S(1)}, f32[32,1,16,128]{3,2,0,1:T(8,128)}, u32[]{:S(2)}) copy-start(f32[32,1,16,128]{3,2,0,1:T(8,128)} %get-tuple-element.25) | copy-start | bytes 786436
  385.2 93.0 %copy-start.4 = (f32[32,1,16,128]{3,2,0,1:T(8,128)S(1)}, f32[32,1,16,128]{3,2,0,1:T(8,128)}, u32[]{:S(2)}) copy-start(f32[32,1,16,128]{3,2,0,1:T(8,128)} %get-tuple-element.55) | copy-start | bytes 786436
  385.2 93.0 %copy-start.5 = (f32[32,1,16,128]{3,2,0,1:T(8,128)S(1)}, f32[32,1,16,128]{3,2,0,1:T(8,128)}, u32[]{:S(2)}) copy-start(f32[32,1,16,128]{3,2,0,1:T(8,128)} %get-tuple-element.50) | copy-start | bytes 786436
  385.2 93.0 %copy-start.6 = (f32[32,1,16,128]{3,2,0,1:T(8,128)S(1)}, f32[32,1,16,128]{3,2,0,1:T(8,128)}, u32[]{:S(2)}) copy-start(f32[32,1,16,128]{3,2,0,1:T(8,128)} %get-tuple-element.51) | copy-start | bytes 786436
  385.2 93.0 %copy-start.7 = (f32[32,1,16,128]{3,2,0,1:T(8,128)S(1)}, f32[32,1,16,128]{3,2,0,1:T(8,128)}, u32[]{:S(2)}) copy-start(f32[32,1,16,128]{3,2,0,1:T(8,128)} %get-tuple-element.46) | copy-start | bytes 786436
  385.2 93.0 %copy-start.8 = (f32[32,1,16,128]{3,2,0,1:T(8,128)S(1)}, f32[32,1,16,128]{3,2,0,1:T(8,128)}, u32[]{:S(2)}) copy-start(f32[32,1,16,128]{3,2,0,1:T(8,128)} %get-tuple-element.47) | copy-start | bytes 786436
  385.2 93.0 %copy-start.9 = (f32[32,1,16,128]{3,2,0,1:T(8,128)S(1)}, f32[32,1,16,128]{3,2,0,1:T(8,128)}, u32[]{:S(2)}) copy-start(f32[32,1,16,128]{3,2,0,1:T(8,128)} %get-tuple-element.42) | copy-start | bytes 786436
  385.2 93.0 %copy-start.10 = (f32[32,1,16,128]{3,2,0,1:T(8,128)S(1)}, f32[32,1,16,128]{3,2,0,1:T(8,128)}, u32[]{:S(2)}) copy-start(f32[32,1,16,128]{3,2,0,1:T(8,128)} %get-tuple-element.43) | copy-start | bytes 786436
  385.2 93.0 %copy-start.11 = (f32[32,1,16,128]{3,2,0,1:T(8,128)S(1)}, f32[32,1,16,128]{3,2,0,1:T(8,128)}, u32[]{:S(2)}) copy-start(f32[32,1,16,128]{3,2,0,1:T(8,128)} %get-tuple-element.38) | copy-start | bytes 786436
  385.3 93.0 %copy-start.12 = (f32[32,1,16,128]{3,2,0,1:T(8,128)S(1)}, f32[32,1,16,128]{3,2,0,1:T(8,128)}, u32[]{:S(2)}) copy-start(f32[32,1,16,128]{3,2,0,1:T(8,128)} %get-tuple-element.39) | copy-start | bytes 786436
  385.3 93.0 %copy-start.13 = (f32[32,1,16,128]{3,2,0,1:T(8,128)S(1)}, f32[32,1,16,128]{3,2,0,1:T(8,128)}, u32[]{:S(2)}) copy-start(f32[32,1,16,128]{3,2,0,1:T(8,128)} %get-tuple-element.34) | copy-start | bytes 786436
  385.3 93.0 %copy-start.14 = (f32[32,1,16,128]{3,2,0,1:T(8,128)S(1)}, f32[32,1,16,128]{3,2,0,1:T(8,128)}, u32[]{:S(2)}) copy-start(f32[32,1,16,128]{3,2,0,1:T(8,128)} %get-tuple-element.35) | copy-start | bytes 786436
where the time goes:
time: 483 us
  blocking collectives  166 us (34%)
  starting transfers between devices  157 us (33%)
  waiting for transfers between devices  92.4 us (19%)
  matrix products  29.5 us (6%)
  other arithmetic  23 us (5%)
  between operations  9.08 us (2%)
  local copies, waits for them, and re-layouts  5.74 us (1%)
    psum x1, blocking collectives, shards(): misfit_total = lax.psum(misfit_sum, ('chan', 'freq'))  166 us
    ppermute x16, starting transfers between devices, shifted(): return lax.ppermute(x, axis, [(i, (i + by) % peers) for i in range(peers)])  157 us
    ppermute x16, waiting for transfers between devices, shifted(): return lax.ppermute(x, axis, [(i, (i + by) % peers) for i in range(peers)])  92.4 us
    dot_general x9, matrix products, pair_terms(): jnp.einsum('xfrc,frd->xfcd', stacked_left, right_rows, preferred_element_...  17.4 us
  transfers between devices with their start and end apart: 16, of which 3 were waited for; matrix products, arithmetic and copies ran while one was open for 11% of the time, Pallas kernels for 0%

commit v1 on v0

--- a/solution.py
+++ b/solution.py
@@ -79,7 +79,7 @@
         misfit_sum = misfit_sum + piece_loss
         adjoint_acc = adjoint_acc + near_terms
         adjoint_acc = adjoint_acc + shifted(far_terms, "chan", s)
-    misfit_total = lax.psum(misfit_sum, ("chan", "freq"))
+    misfit_total = lax.all_gather(misfit_sum, axis_name=("chan", "freq")).sum(axis=0)
     misfit = misfit_total / float(F * block_width * block_total * BAND)
     return (adjoint_acc * (1.0 / W), misfit)
 

time: 483 us -> 495 us (1.025)
  the two profiles are of different devices: /device:TPU:104 before, /device:TPU:192 now
where the time goes in v1:
time: 495 us; the launch traced here: 494 us
  waiting for transfers between devices  190 us (38%)
  starting transfers between devices  115 us (23%)
  blocking collectives  115 us (23%)
  matrix products  29.5 us (6%)
  other arithmetic  25.6 us (5%)
  local copies, waits for them, and re-layouts  9.82 us (2%)
  between operations  9.13 us (2%)
    ppermute x16, waiting for transfers between devices, shifted(): return lax.ppermute(x, axis, [(i, (i + by) % peers) for i in range(peers)])  190 us
    ppermute x16, starting transfers between devices, shifted(): return lax.ppermute(x, axis, [(i, (i + by) % peers) for i in range(peers)])  115 us
    unnamed x1, blocking collectives  115 us
    dot_general x9, matrix products, pair_terms(): jnp.einsum('xfrc,frd->xfcd', stacked_left, right_rows, preferred_element_...  17.4 us
  transfers between devices with their start and end apart: 16, of which 5 were waited for; matrix products, arithmetic and copies ran while one was open for 12% of the time, Pallas kernels for 0%

profile of v1, /device:TPU:192, one launch (start us, length us, event | category | flops | bytes accessed | tf_op | source)
XLA Modules:
  0.0 493.8 jit_solution(9536088443471651797)
XLA Ops:
  0.7 1.0 constant_dynamic-update-slice_fusion.1
  1.6 0.9 constant_dynamic-update-slice_fusion
  2.6 1.4 broadcast_multiply_fusion
  4.0 7.4 %collective-permute-start.14 = (bf16[32,2,24,128]{3,2,0,1:T(8,128)(2,1)}, bf16[32,2,24,128]{3,2,0,1:T(8,128)(2,1)}, u32[]{:S(2)}, u32[]{:S(2)}) collective-permute-start(bf16[32,2,24,128]{3,2,0,1:T(8,128)(2,1)} %get-tuple-element.61), channel_id=1, source_target_pairs={{0,448},{8,456},{16,464},{24,472},{32,480},{40,488},{48,496},{56,5... | collective-permute-start | bytes 1179656 | tf_op jit(solution)/shard_map/ppermute | solution.py:13
  11.4 1.9 collective-permute-start.12
  13.3 11.4 %collective-permute-start.10 = (bf16[32,2,24,128]{3,2,0,1:T(8,128)(2,1)}, bf16[32,2,24,128]{3,2,0,1:T(8,128)(2,1)S(1)}, u32[]{:S(2)}, u32[]{:S(2)}) collective-permute-start(bf16[32,2,24,128]{3,2,0,1:T(8,128)(2,1)} %get-tuple-element.61), channel_id=1, source_target_pairs={{0,464},{8,472},{16,480},{24,488},{32,496},{40,504},{48,0},{56,8},... | collective-permute-start | bytes 1179656 | tf_op jit(solution)/shard_map/ppermute | solution.py:13
  24.8 12.3 %collective-permute-start.8 = (bf16[32,2,24,128]{3,2,0,1:T(8,128)(2,1)}, bf16[32,2,24,128]{3,2,0,1:T(8,128)(2,1)S(1)}, u32[]{:S(2)}, u32[]{:S(2)}) collective-permute-start(bf16[32,2,24,128]{3,2,0,1:T(8,128)(2,1)} %get-tuple-element.61), channel_id=1, source_target_pairs={{0,472},{8,480},{16,488},{24,496},{32,504},{40,0},{48,8},{56,16},{... | collective-permute-start | bytes 1179656 | tf_op jit(solution)/shard_map/ppermute | solution.py:13
  37.1 3.0 collective-permute-start.6
  41.4 1.8 multiply_select_fusion.8
  43.2 2.0 multiply_reduce_fusion.8
  45.2 0.8 fusion.91
  47.9 0.9 fusion.144
  48.7 1.9 collective-permute-start.4
  50.7 1.0 copy.99
  51.7 1.9 multiply_reduce_fusion
  53.6 0.8 fusion.88
  54.4 1.0 slice.417
  56.0 0.9 fusion.114
  56.8 39.9 %collective-permute-done.12 = bf16[32,2,24,128]{3,2,0,1:T(8,128)(2,1)} collective-permute-done((bf16[32,2,24,128]{3,2,0,1:T(8,128)(2,1)}, bf16[32,2,24,128]{3,2,0,1:T(8,128)(2,1)}, u32[]{:S(2)}, u32[]{:S(2)}) %collective-permute-start.12) | collective-permute-done | bytes 393248 | tf_op jit(solution)/shard_map/ppermute | solution.py:13
  96.8 1.9 collective-permute-start.2
  98.7 1.0 copy.93
  99.7 2.0 multiply_reduce_fusion.1
  102.5 1.0 slice.408
  104.0 0.9 fusion.118
  104.9 37.2 %collective-permute-start = (bf16[32,2,24,128]{3,2,0,1:T(8,128)(2,1)}, bf16[32,2,24,128]{3,2,0,1:T(8,128)(2,1)S(1)}, u32[]{:S(2)}, u32[]{:S(2)}) collective-permute-start(bf16[32,2,24,128]{3,2,0,1:T(8,128)(2,1)} %get-tuple-element.61), channel_id=1, source_target_pairs={{0,504},{8,0},{16,8},{24,16},{32,24},{40,32},{48,40},{56,48},{64,5... | collective-permute-start | bytes 1179656 | tf_op jit(solution)/shard_map/ppermute | solution.py:13
  142.1 2.0 multiply_reduce_fusion.2
  144.1 0.8 fusion.76
  145.5 0.8 pad_maximum_fusion.8
  147.1 57.2 %collective-permute-done.8 = bf16[32,2,24,128]{3,2,0,1:T(8,128)(2,1)S(1)} collective-permute-done((bf16[32,2,24,128]{3,2,0,1:T(8,128)(2,1)}, bf16[32,2,24,128]{3,2,0,1:T(8,128)(2,1)S(1)}, u32[]{:S(2)}, u32[]{:S(2)}) %collective-permute-start.8) | collective-permute-done | bytes 393248 | tf_op jit(solution)/shard_map/ppermute | solution.py:13
  204.3 2.1 collective-permute-start.15
  206.5 2.0 multiply_reduce_fusion.3
  208.5 0.8 fusion.70
  209.8 0.8 pad_maximum_fusion.7
  211.5 1.9 collective-permute-start.13
  213.4 1.9 multiply_reduce_fusion.4
  215.3 0.8 fusion.64
  216.7 0.9 pad_maximum_fusion.6
  218.3 16.0 %collective-permute-start.11 = (f32[32,2,16,128]{3,2,0,1:T(8,128)}, f32[32,2,16,128]{3,2,0,1:T(8,128)}, u32[]{:S(2)}, u32[]{:S(2)}) collective-permute-start(f32[32,2,16,128]{3,2,0,1:T(8,128)} %pad_maximum_fusion.6), channel_id=1, source_target_pairs={{0,48},{8,56},{16,64},{24,72},{32,80},{40,88},{48,96},{56,104},{64... | collective-permute-start | bytes 1572872 | tf_op jit(solution)/shard_map/ppermute | solution.py:13
  234.4 1.9 multiply_reduce_fusion.5
  236.3 0.8 fusion.58
  237.2 0.9 fusion.132
  238.1 0.8 pad_maximum_fusion.5
  239.4 1.9 collective-permute-start.9
  241.4 1.9 multiply_reduce_fusion.6
  244.1 0.9 fusion.134
  245.7 0.8 pad_maximum_fusion.4
  246.5 0.9 fusion.136
  247.5 1.9 collective-permute-start.7
  249.4 1.9 multiply_reduce_fusion.7
  251.3 0.8 fusion.46
  252.1 0.9 fusion.140
  259.6 114.6 %all-reduce = f32[512]{0:T(512)S(1)} all-reduce(f32[512]{0:T(512)S(1)} %dynamic-update-slice), channel_id=1, replica_groups=mesh['chan'=64,'freq'=8] {'chan','freq'}, use_global_device_ids=true, to_apply=%add | all-reduce | flops 512 | bytes 4096
  374.7 1.8 pad_maximum_fusion.3
  376.6 1.9 pad_maximum_fusion.2
  378.5 0.9 pad_maximum_fusion.1
  380.1 1.5 fusion.49
  381.7 4.4 collective-permute-start.5
  386.1 8.1 %collective-permute-start.3 = (f32[32,2,16,128]{3,2,0,1:T(8,128)S(1)}, f32[32,2,16,128]{3,2,0,1:T(8,128)S(1)}, u32[]{:S(2)}, u32[]{:S(2)}) collective-permute-start(f32[32,2,16,128]{3,2,0,1:T(8,128)S(1)} %copy-done.21), channel_id=1, source_target_pairs={{0,16},{8,24},{16,32},{24,40},{32,48},{40,56},{48,64},{56,72},{64,... | collective-permute-start | bytes 1572872 | tf_op jit(solution)/shard_map/ppermute | solution.py:13
  394.2 1.9 collective-permute-start.1
  396.8 23.7 %collective-permute-done.5 = f32[32,2,16,128]{3,2,0,1:T(8,128)S(1)} collective-permute-done((f32[32,2,16,128]{3,2,0,1:T(8,128)S(1)}, f32[32,2,16,128]{3,2,0,1:T(8,128)S(1)}, u32[]{:S(2)}, u32[]{:S(2)}) %collective-permute-start.5) | collective-permute-done | bytes 524320 | tf_op jit(solution)/shard_map/ppermute | solution.py:13
  420.5 67.7 %collective-permute-done.3 = f32[32,2,16,128]{3,2,0,1:T(8,128)S(1)} collective-permute-done((f32[32,2,16,128]{3,2,0,1:T(8,128)S(1)}, f32[32,2,16,128]{3,2,0,1:T(8,128)S(1)}, u32[]{:S(2)}, u32[]{:S(2)}) %collective-permute-start.3) | collective-permute-done | bytes 524320 | tf_op jit(solution)/shard_map/ppermute | solution.py:13
  488.2 1.2 collective-permute-done.1
  489.5 2.3 fusion.110
  491.8 0.9 copy.104
  (144 shorter events, 13.0 us)
Async XLA Ops:
  0.6 39.8 %copy-start.36 = (bf16[24]{0:T(256)(128)(2,1)S(1)}, bf16[24]{0:T(256)(128)(2,1)}, u32[]{:S(2)}) copy-start(bf16[24]{0:T(256)(128)(2,1)} %constant.88.clone.1) | copy-start | bytes 148
  0.6 39.7 %copy-start.35 = (s32[8192]{0:T(1024)S(1)}, s32[8192]{0:T(1024)}, u32[]{:S(2)}) copy-start(s32[8192]{0:T(1024)} %param.6) | copy-start | bytes 98308
  0.7 39.8 %copy-start.37 = (s32[64]{0:T(128)S(1)}, s32[64]{0:T(128)}, u32[]{:S(2)}) copy-start(s32[64]{0:T(128)} %param.7) | copy-start | bytes 772
  4.0 44.7 %collective-permute-start.14 = (bf16[32,2,24,128]{3,2,0,1:T(8,128)(2,1)}, bf16[32,2,24,128]{3,2,0,1:T(8,128)(2,1)}, u32[]{:S(2)}, u32[]{:S(2)}) collective-permute-start(bf16[32,2,24,128]{3,2,0,1:T(8,128)(2,1)} %get-tuple-element.61), channel_id=1, source_target_pairs={{0,448},{8,456},{16,464},{24,472},{32,480},{40,488},{48,496},{56,5... | collective-permute-start | bytes 1179656 | tf_op jit(solution)/shard_map/ppermute | solution.py:13
  11.4 85.4 %collective-permute-start.12 = (bf16[32,2,24,128]{3,2,0,1:T(8,128)(2,1)}, bf16[32,2,24,128]{3,2,0,1:T(8,128)(2,1)}, u32[]{:S(2)}, u32[]{:S(2)}) collective-permute-start(bf16[32,2,24,128]{3,2,0,1:T(8,128)(2,1)} %get-tuple-element.61), channel_id=1, source_target_pairs={{0,456},{8,464},{16,472},{24,480},{32,488},{40,496},{48,504},{56,0... | collective-permute-start | bytes 1179656 | tf_op jit(solution)/shard_map/ppermute | solution.py:13
  13.3 91.6 %collective-permute-start.10 = (bf16[32,2,24,128]{3,2,0,1:T(8,128)(2,1)}, bf16[32,2,24,128]{3,2,0,1:T(8,128)(2,1)S(1)}, u32[]{:S(2)}, u32[]{:S(2)}) collective-permute-start(bf16[32,2,24,128]{3,2,0,1:T(8,128)(2,1)} %get-tuple-element.61), channel_id=1, source_target_pairs={{0,464},{8,472},{16,480},{24,488},{32,496},{40,504},{48,0},{56,8},... | collective-permute-start | bytes 1179656 | tf_op jit(solution)/shard_map/ppermute | solution.py:13
  24.8 179.6 %collective-permute-start.8 = (bf16[32,2,24,128]{3,2,0,1:T(8,128)(2,1)}, bf16[32,2,24,128]{3,2,0,1:T(8,128)(2,1)S(1)}, u32[]{:S(2)}, u32[]{:S(2)}) collective-permute-start(bf16[32,2,24,128]{3,2,0,1:T(8,128)(2,1)} %get-tuple-element.61), channel_id=1, source_target_pairs={{0,472},{8,480},{16,488},{24,496},{32,504},{40,0},{48,8},{56,16},{... | collective-permute-start | bytes 1179656 | tf_op jit(solution)/shard_map/ppermute | solution.py:13
  37.1 174.4 %collective-permute-start.6 = (bf16[32,2,24,128]{3,2,0,1:T(8,128)(2,1)}, bf16[32,2,24,128]{3,2,0,1:T(8,128)(2,1)S(1)}, u32[]{:S(2)}, u32[]{:S(2)}) collective-permute-start(bf16[32,2,24,128]{3,2,0,1:T(8,128)(2,1)} %get-tuple-element.61), channel_id=1, source_target_pairs={{0,480},{8,488},{16,496},{24,504},{32,0},{40,8},{48,16},{56,24},{6... | collective-permute-start | bytes 1179656 | tf_op jit(solution)/shard_map/ppermute | solution.py:13
  41.1 4.0 copy-start.23
  41.2 3.9 copy-start.25
  43.2 2.0 copy-start
  47.2 4.6 copy-start.24
  47.2 4.6 copy-start.26
  47.2 4.6 copy-start.34
  48.7 169.6 %collective-permute-start.4 = (bf16[32,2,24,128]{3,2,0,1:T(8,128)(2,1)}, bf16[32,2,24,128]{3,2,0,1:T(8,128)(2,1)S(1)}, u32[]{:S(2)}, u32[]{:S(2)}) collective-permute-start(bf16[32,2,24,128]{3,2,0,1:T(8,128)(2,1)} %get-tuple-element.61), channel_id=1, source_target_pairs={{0,488},{8,496},{16,504},{24,0},{32,8},{40,16},{48,24},{56,32},{64... | collective-permute-start | bytes 1179656 | tf_op jit(solution)/shard_map/ppermute | solution.py:13
  55.9 43.9 %copy-start.33 = (f32[128,128]{0,1:T(8,128)S(1)}, f32[128,128]{0,1:T(8,128)}, u32[]{:S(2)}) copy-start(f32[128,128]{0,1:T(8,128)} %get-tuple-element.77) | copy-start | bytes 196612
  96.8 142.6 %collective-permute-start.2 = (bf16[32,2,24,128]{3,2,0,1:T(8,128)(2,1)}, bf16[32,2,24,128]{3,2,0,1:T(8,128)(2,1)S(1)}, u32[]{:S(2)}, u32[]{:S(2)}) collective-permute-start(bf16[32,2,24,128]{3,2,0,1:T(8,128)(2,1)} %get-tuple-element.61), channel_id=1, source_target_pairs={{0,496},{8,504},{16,0},{24,8},{32,16},{40,24},{48,32},{56,40},{64,... | collective-permute-start | bytes 1179656 | tf_op jit(solution)/shard_map/ppermute | solution.py:13
  103.9 38.2 %copy-start.32 = (f32[128,128]{0,1:T(8,128)S(1)}, f32[128,128]{0,1:T(8,128)}, u32[]{:S(2)}) copy-start(f32[128,128]{0,1:T(8,128)} %get-tuple-element.76) | copy-start | bytes 196612
  104.9 142.6 %collective-permute-start = (bf16[32,2,24,128]{3,2,0,1:T(8,128)(2,1)}, bf16[32,2,24,128]{3,2,0,1:T(8,128)(2,1)S(1)}, u32[]{:S(2)}, u32[]{:S(2)}) collective-permute-start(bf16[32,2,24,128]{3,2,0,1:T(8,128)(2,1)} %get-tuple-element.61), channel_id=1, source_target_pairs={{0,504},{8,0},{16,8},{24,16},{32,24},{40,32},{48,40},{56,48},{64,5... | collective-permute-start | bytes 1179656 | tf_op jit(solution)/shard_map/ppermute | solution.py:13
  145.5 61.0 %copy-start.31 = (f32[128,128]{0,1:T(8,128)S(1)}, f32[128,128]{0,1:T(8,128)}, u32[]{:S(2)}) copy-start(f32[128,128]{0,1:T(8,128)} %get-tuple-element.75) | copy-start | bytes 196612
  204.3 177.3 %collective-permute-start.15 = (f32[32,2,16,128]{3,2,0,1:T(8,128)}, f32[32,2,16,128]{3,2,0,1:T(8,128)}, u32[]{:S(2)}, u32[]{:S(2)}) collective-permute-start(f32[32,2,16,128]{3,2,0,1:T(8,128)} %pad_maximum_fusion.8), channel_id=1, source_target_pairs={{0,64},{8,72},{16,80},{24,88},{32,96},{40,104},{48,112},{56,120},{... | collective-permute-start | bytes 1572872 | tf_op jit(solution)/shard_map/ppermute | solution.py:13
  209.8 3.6 copy-start.30
  211.5 174.6 %collective-permute-start.13 = (f32[32,2,16,128]{3,2,0,1:T(8,128)}, f32[32,2,16,128]{3,2,0,1:T(8,128)}, u32[]{:S(2)}, u32[]{:S(2)}) collective-permute-start(f32[32,2,16,128]{3,2,0,1:T(8,128)} %pad_maximum_fusion.7), channel_id=1, source_target_pairs={{0,56},{8,64},{16,72},{24,80},{32,88},{40,96},{48,104},{56,112},{6... | collective-permute-start | bytes 1572872 | tf_op jit(solution)/shard_map/ppermute | solution.py:13
  216.7 17.7 %copy-start.29 = (f32[128,128]{0,1:T(8,128)S(1)}, f32[128,128]{0,1:T(8,128)}, u32[]{:S(2)}) copy-start(f32[128,128]{0,1:T(8,128)} %get-tuple-element.73) | copy-start | bytes 196612
  218.3 175.9 %collective-permute-start.11 = (f32[32,2,16,128]{3,2,0,1:T(8,128)}, f32[32,2,16,128]{3,2,0,1:T(8,128)}, u32[]{:S(2)}, u32[]{:S(2)}) collective-permute-start(f32[32,2,16,128]{3,2,0,1:T(8,128)} %pad_maximum_fusion.6), channel_id=1, source_target_pairs={{0,48},{8,56},{16,64},{24,72},{32,80},{40,88},{48,96},{56,104},{64... | collective-permute-start | bytes 1572872 | tf_op jit(solution)/shard_map/ppermute | solution.py:13
  239.0 2.4 copy-start.28
  239.4 157.4 %collective-permute-start.9 = (f32[32,2,16,128]{3,2,0,1:T(8,128)}, f32[32,2,16,128]{3,2,0,1:T(8,128)}, u32[]{:S(2)}, u32[]{:S(2)}) collective-permute-start(f32[32,2,16,128]{3,2,0,1:T(8,128)} %pad_maximum_fusion.5), channel_id=1, source_target_pairs={{0,40},{8,48},{16,56},{24,64},{32,72},{40,80},{48,88},{56,96},{64,... | collective-permute-start | bytes 1572872 | tf_op jit(solution)/shard_map/ppermute | solution.py:13
  245.0 4.5 copy-start.27
  247.5 149.3 %collective-permute-start.7 = (f32[32,2,16,128]{3,2,0,1:T(8,128)}, f32[32,2,16,128]{3,2,0,1:T(8,128)}, u32[]{:S(2)}, u32[]{:S(2)}) collective-permute-start(f32[32,2,16,128]{3,2,0,1:T(8,128)} %pad_maximum_fusion.4), channel_id=1, source_target_pairs={{0,32},{8,40},{16,48},{24,56},{32,64},{40,72},{48,80},{56,88},{64,... | collective-permute-start | bytes 1572872 | tf_op jit(solution)/shard_map/ppermute | solution.py:13
  251.3 1.7 copy-start.1
  252.1 122.6 %copy-start.16 = (f32[32,1,16,128]{3,2,0,1:T(8,128)S(1)}, f32[32,1,16,128]{3,2,0,1:T(8,128)}, u32[]{:S(2)}) copy-start(f32[32,1,16,128]{3,2,0,1:T(8,128)} %get-tuple-element.36) | copy-start | bytes 786436
  374.7 3.7 copy-start.17
  374.7 3.7 copy-start.18
  380.0 1.6 copy-start.20
  380.0 6.1 %copy-start.21 = (f32[32,2,16,128]{3,2,0,1:T(8,128)S(1)}, f32[32,2,16,128]{3,2,0,1:T(8,128)}, u32[]{:S(2)}) copy-start(f32[32,2,16,128]{3,2,0,1:T(8,128)} %pad_maximum_fusion.2) | copy-start | bytes 1572868
  380.0 14.2 %copy-start.22 = (f32[32,2,16,128]{3,2,0,1:T(8,128)S(1)}, f32[32,2,16,128]{3,2,0,1:T(8,128)}, u32[]{:S(2)}) copy-start(f32[32,2,16,128]{3,2,0,1:T(8,128)} %pad_maximum_fusion.1) | copy-start | bytes 1572868
  380.0 16.1 %copy-start.2 = (bf16[2,32,128,128]{2,3,0,1:T(8,128)(2,1)S(1)}, bf16[2,32,128,128]{2,3,0,1:T(8,128)(2,1)}, u32[]{:S(2)}) copy-start(bf16[2,32,128,128]{2,3,0,1:T(8,128)(2,1)} %copy-done.1) | copy-start | bytes 6291460
  380.1 16.1 %copy-start.19 = (bf16[32,2,16,128]{3,2,1,0:T(8,128)(2,1)S(1)}, bf16[32,2,16,128]{3,2,1,0:T(8,128)(2,1)}, u32[]{:S(2)}) copy-start(bf16[32,2,16,128]{3,2,1,0:T(8,128)(2,1)} %copy.56) | copy-start | bytes 786436
  381.7 38.9 %collective-permute-start.5 = (f32[32,2,16,128]{3,2,0,1:T(8,128)S(1)}, f32[32,2,16,128]{3,2,0,1:T(8,128)S(1)}, u32[]{:S(2)}, u32[]{:S(2)}) collective-permute-start(f32[32,2,16,128]{3,2,0,1:T(8,128)S(1)} %copy-done.20), channel_id=1, source_target_pairs={{0,24},{8,32},{16,40},{24,48},{32,56},{40,64},{48,72},{56,80},{64,... | collective-permute-start | bytes 1572872 | tf_op jit(solution)/shard_map/ppermute | solution.py:13
  386.1 102.1 %collective-permute-start.3 = (f32[32,2,16,128]{3,2,0,1:T(8,128)S(1)}, f32[32,2,16,128]{3,2,0,1:T(8,128)S(1)}, u32[]{:S(2)}, u32[]{:S(2)}) collective-permute-start(f32[32,2,16,128]{3,2,0,1:T(8,128)S(1)} %copy-done.21), channel_id=1, source_target_pairs={{0,16},{8,24},{16,32},{24,40},{32,48},{40,56},{48,64},{56,72},{64,... | collective-permute-start | bytes 1572872 | tf_op jit(solution)/shard_map/ppermute | solution.py:13
  394.2 95.2 %collective-permute-start.1 = (f32[32,2,16,128]{3,2,0,1:T(8,128)S(1)}, f32[32,2,16,128]{3,2,0,1:T(8,128)S(1)}, u32[]{:S(2)}, u32[]{:S(2)}) collective-permute-start(f32[32,2,16,128]{3,2,0,1:T(8,128)S(1)} %copy-done.22), channel_id=1, source_target_pairs={{0,8},{8,16},{16,24},{24,32},{32,40},{40,48},{48,56},{56,64},{64,7... | collective-permute-start | bytes 1572872 | tf_op jit(solution)/shard_map/ppermute | solution.py:13
  396.2 93.3 %copy-start.3 = (f32[32,1,16,128]{3,2,0,1:T(8,128)S(1)}, f32[32,1,16,128]{3,2,0,1:T(8,128)}, u32[]{:S(2)}) copy-start(f32[32,1,16,128]{3,2,0,1:T(8,128)} %fusion.145) | copy-start | bytes 786436
  396.2 93.2 %copy-start.4 = (f32[32,1,16,128]{3,2,0,1:T(8,128)S(1)}, f32[32,1,16,128]{3,2,0,1:T(8,128)}, u32[]{:S(2)}) copy-start(f32[32,1,16,128]{3,2,0,1:T(8,128)} %fusion.147) | copy-start | bytes 786436
  396.2 93.2 %copy-start.5 = (f32[32,1,16,128]{3,2,0,1:T(8,128)S(1)}, f32[32,1,16,128]{3,2,0,1:T(8,128)}, u32[]{:S(2)}) copy-start(f32[32,1,16,128]{3,2,0,1:T(8,128)} %get-tuple-element.24) | copy-start | bytes 786436
  396.2 93.2 %copy-start.6 = (f32[32,1,16,128]{3,2,0,1:T(8,128)S(1)}, f32[32,1,16,128]{3,2,0,1:T(8,128)}, u32[]{:S(2)}) copy-start(f32[32,1,16,128]{3,2,0,1:T(8,128)} %get-tuple-element.25) | copy-start | bytes 786436
  396.2 93.2 %copy-start.7 = (f32[32,1,16,128]{3,2,0,1:T(8,128)S(1)}, f32[32,1,16,128]{3,2,0,1:T(8,128)}, u32[]{:S(2)}) copy-start(f32[32,1,16,128]{3,2,0,1:T(8,128)} %get-tuple-element.54) | copy-start | bytes 786436
  396.2 93.2 %copy-start.8 = (f32[32,1,16,128]{3,2,0,1:T(8,128)S(1)}, f32[32,1,16,128]{3,2,0,1:T(8,128)}, u32[]{:S(2)}) copy-start(f32[32,1,16,128]{3,2,0,1:T(8,128)} %get-tuple-element.55) | copy-start | bytes 786436
  396.2 93.2 %copy-start.9 = (f32[32,1,16,128]{3,2,0,1:T(8,128)S(1)}, f32[32,1,16,128]{3,2,0,1:T(8,128)}, u32[]{:S(2)}) copy-start(f32[32,1,16,128]{3,2,0,1:T(8,128)} %get-tuple-element.50) | copy-start | bytes 786436
  396.2 93.2 %copy-start.10 = (f32[32,1,16,128]{3,2,0,1:T(8,128)S(1)}, f32[32,1,16,128]{3,2,0,1:T(8,128)}, u32[]{:S(2)}) copy-start(f32[32,1,16,128]{3,2,0,1:T(8,128)} %get-tuple-element.51) | copy-start | bytes 786436
  396.2 93.2 %copy-start.11 = (f32[32,1,16,128]{3,2,0,1:T(8,128)S(1)}, f32[32,1,16,128]{3,2,0,1:T(8,128)}, u32[]{:S(2)}) copy-start(f32[32,1,16,128]{3,2,0,1:T(8,128)} %get-tuple-element.47) | copy-start | bytes 786436
  396.2 93.2 %copy-start.12 = (f32[32,1,16,128]{3,2,0,1:T(8,128)S(1)}, f32[32,1,16,128]{3,2,0,1:T(8,128)}, u32[]{:S(2)}) copy-start(f32[32,1,16,128]{3,2,0,1:T(8,128)} %get-tuple-element.43) | copy-start | bytes 786436
  396.3 93.2 %copy-start.13 = (f32[32,1,16,128]{3,2,0,1:T(8,128)S(1)}, f32[32,1,16,128]{3,2,0,1:T(8,128)}, u32[]{:S(2)}) copy-start(f32[32,1,16,128]{3,2,0,1:T(8,128)} %get-tuple-element.39) | copy-start | bytes 786436
  396.3 93.2 %copy-start.14 = (f32[32,1,16,128]{3,2,0,1:T(8,128)S(1)}, f32[32,1,16,128]{3,2,0,1:T(8,128)}, u32[]{:S(2)}) copy-start(f32[32,1,16,128]{3,2,0,1:T(8,128)} %get-tuple-element.34) | copy-start | bytes 786436
  396.3 93.2 %copy-start.15 = (f32[32,1,16,128]{3,2,0,1:T(8,128)S(1)}, f32[32,1,16,128]{3,2,0,1:T(8,128)}, u32[]{:S(2)}) copy-start(f32[32,1,16,128]{3,2,0,1:T(8,128)} %get-tuple-element.35) | copy-start | bytes 786436
